TPU v7x, 32 devices: a whole 2x2x4 slice. The times are simulated.
32 devices in a mesh: grp: 4 (over x, core), ep: 4 (over z), sq: 2 (over y).
Axes of the slice: x: 2, y: 2, z: 4, core: 2. Of those that a mesh axis runs over, the one named last changes fastest.
Arguments:
- queries: bfloat16 [8192, 2048], P(('grp', 'ep', 'sq')), may hold values from -32 to 32
- keys: bfloat16 [8192, 512], P(('grp', 'ep', 'sq')), may hold values from -32 to 32
- values: bfloat16 [8192, 512], P(('grp', 'ep', 'sq')), may hold values from -6 to 6
- norm_gain: float32 [2048], replicated, may hold values from 0.1 to 1.9
- expert_ids: int32 [8192, 2], P(('grp', 'ep', 'sq')), may hold values from 0 to 3, all different within a row; in each aligned block of 256 rows (0 to 255, 256 to 511, ...) at most 192 rows name the same one
- gate_values: float32 [8192, 2], P(('grp', 'ep', 'sq')), may hold values from 0.1 to 1
- hidden_grad: bfloat16 [8192, 1024], P(('grp', 'ep', 'sq')), may hold values from -0.59765625 to 0.59765625
- gate_weight: bfloat16 [4, 2048, 1024], P('ep', None, 'sq'), may hold values from -0.125 to 0.125
- up_weight: bfloat16 [4, 2048, 1024], P('ep', None, 'sq'), may hold values from -0.125 to 0.125
Outputs:
- gate_grad: float32 [4, 2048, 1024], P('ep', 'grp', 'sq')
Inputs may be any that keep to these rules, and one draw needn't show every extreme that they name: `expert_ids`: each token names 2 different experts; within the 256 tokens of one device no expert is named more than 192 times.
All inputs are finite; a program needn't handle non-finite values.
Results may differ from a plain program's by a relative error of at most 0.0085.
Values may be sent and summed in bfloat16 or wider, within the bound.
A program may use at most 64 MiB of HBM per device.

v0:
```python
import math
import jax
import jax.numpy as jnp
from jax import lax
from jax.sharding import PartitionSpec as P

HEAD_DIM = 128
LENGTH = 512
epsilon = 1e-05
masked_score = -1e30


def gate_term(inputs, cotangent, weight_gate, weight_up):
    pre_gate = jnp.dot(inputs, weight_gate, preferred_element_type=jnp.float32)
    pre_up = jnp.dot(inputs, weight_up, preferred_element_type=jnp.float32)
    sigmoid_gate = jax.nn.sigmoid(pre_gate)
    slope = sigmoid_gate * (1.0 + pre_gate * (1.0 - sigmoid_gate))
    delta_gate = (cotangent.astype(jnp.float32) * pre_up * slope).astype(jnp.bfloat16)
    return lax.dot_general(
        inputs, delta_gate, (((0,), (0,)), ((), ())), preferred_element_type=jnp.float32
    )


def body(
    queries, keys, values, norm_gain, expert_ids, gate_values, hidden_grad, gate_weight, up_weight
):
    rows_here, model_width = queries.shape
    kv_width = keys.shape[1]
    kv_heads = kv_width // HEAD_DIM
    group_size = model_width // kv_width
    score_scale = 1.0 / math.sqrt(HEAD_DIM)
    shard_index = lax.axis_index("sq")
    query_positions = shard_index * rows_here + jnp.arange(rows_here, dtype=jnp.int32)
    query_sequence = query_positions // LENGTH
    query_heads = queries.reshape(rows_here, kv_heads, group_size, HEAD_DIM)
    running_max = jnp.full((rows_here, kv_heads, group_size), masked_score, jnp.float32)
    key_rows = lax.all_gather(keys, "sq", axis=0, tiled=True)
    value_rows = lax.all_gather(values, "sq", axis=0, tiled=True)
    key_count = key_rows.shape[0]
    key_heads = key_rows.reshape(key_count, kv_heads, HEAD_DIM)
    value_heads = value_rows.reshape(key_count, kv_heads, HEAD_DIM)
    scores = (
        jnp.einsum("tkgd,rkd->tkgr", query_heads, key_heads, preferred_element_type=jnp.float32)
        * score_scale
    )
    key_positions = jnp.arange(key_count, dtype=jnp.int32)
    causal = key_positions[None, :] <= query_positions[:, None]
    same_sequence = (key_positions // LENGTH)[None, :] == query_sequence[:, None]
    allowed = (causal & same_sequence)[:, None, None, :]
    scores = jnp.where(allowed, scores, masked_score)
    updated_max = jnp.maximum(running_max, jnp.max(scores, axis=-1))
    exponent_terms = jnp.where(allowed, jnp.exp(scores - updated_max[..., None]), 0.0)
    running_sum = jnp.sum(exponent_terms, axis=-1)
    running_out = jnp.einsum(
        "tkgr,rkd->tkgd",
        exponent_terms.astype(jnp.bfloat16),
        value_heads,
        preferred_element_type=jnp.float32,
    )
    attended = (running_out / running_sum[..., None]).reshape(rows_here, model_width)
    mean_square = jnp.mean(attended * attended, axis=-1, keepdims=True)
    normed = (attended * lax.rsqrt(mean_square + epsilon) * norm_gain).astype(jnp.bfloat16)
    top_count = expert_ids.shape[1]
    experts = lax.axis_size("ep")
    capacity = rows_here * top_count // experts * 3 // 2
    hidden_width = hidden_grad.shape[1]
    flat_ids = expert_ids.reshape(-1)
    one_hot = (flat_ids[:, None] == jnp.arange(experts, dtype=jnp.int32)[None, :]).astype(jnp.int32)
    slot_rank = jnp.sum(jnp.cumsum(one_hot, axis=0) * one_hot, axis=1) - 1
    slot_target = flat_ids * capacity + slot_rank
    routed_inputs = jnp.repeat(normed, top_count, axis=0)
    routed_grad = (
        gate_values.reshape(-1, 1) * jnp.repeat(hidden_grad, top_count, axis=0).astype(jnp.float32)
    ).astype(jnp.bfloat16)
    send_inputs = (
        jnp.zeros((experts * capacity, model_width), jnp.bfloat16)
        .at[slot_target]
        .set(routed_inputs)
    )
    send_grad = (
        jnp.zeros((experts * capacity, hidden_width), jnp.bfloat16).at[slot_target].set(routed_grad)
    )
    send_inputs = send_inputs.reshape(experts, capacity, model_width)
    send_grad = send_grad.reshape(experts, capacity, hidden_width)
    got_inputs, got_grad = (
        lax.all_to_all(send_inputs, "ep", split_axis=0, concat_axis=0, tiled=True),
        lax.all_to_all(send_grad, "ep", split_axis=0, concat_axis=0, tiled=True),
    )
    expert_inputs = got_inputs.reshape(-1, model_width)
    expert_grad = got_grad.reshape(-1, hidden_width)
    weight_gate = gate_weight[0]
    weight_up = up_weight[0]
    local_hidden = weight_gate.shape[1]
    column_start = shard_index * local_hidden
    input_rows = lax.all_gather(expert_inputs, "sq", axis=0, tiled=True)
    grad_rows = lax.all_gather(expert_grad, "sq", axis=0, tiled=True)
    cotangent = lax.dynamic_slice_in_dim(grad_rows, column_start, local_hidden, 1)
    summed = gate_term(input_rows, cotangent, weight_gate, weight_up)
    return lax.psum_scatter(
        summed[None].astype(jnp.bfloat16), "grp", scatter_dimension=1, tiled=True
    ).astype(jnp.float32)


def solution(mesh):
    return jax.shard_map(
        body,
        mesh=mesh,
        in_specs=(
            P(("grp", "ep", "sq"), None),
            P(("grp", "ep", "sq"), None),
            P(("grp", "ep", "sq"), None),
            P(),
            P(("grp", "ep", "sq"), None),
            P(("grp", "ep", "sq"), None),
            P(("grp", "ep", "sq"), None),
            P("ep", None, "sq"),
            P("ep", None, "sq"),
        ),
        out_specs=P("ep", "grp", "sq"),
        check_vma=False,
    )
```

profile of v0, /device:TPU:0, one launch (start us, length us, event | category | flops | bytes accessed | tf_op | source)
XLA Modules:
  0.0 312.1 jit_solution(6690040816627483020)
XLA Ops:
  6.5 0.0 copy-start
  6.5 0.0 all-gather.3.cloned.1.call-start
  6.5 0.8 broadcast_multiply_fusion
  7.4 0.8 copy.15
  8.2 0.1 eq.46
  8.3 0.1 eq.42
  8.5 0.1 copy.14
  8.6 0.1 mul.78
  8.8 1.2 reduce-window.6
  10.0 0.2 slice_reduce_fusion
  10.2 0.2 reduce-window.9
  10.4 0.1 add_bitcast_fusion
  10.5 1.1 copy.17
  11.6 10.0 %all_gather.12 = bf16[512,512]{0,1:T(8,128)(2,1)} all-gather(bf16[256,512]{0,1:T(8,128)(2,1)S(1)} %copy.17), channel_id=1, replica_groups=mesh['grp'=4,'ep'=4,'sq'=2] {'sq'}, dimensions={0}, use_global_device_ids=true | all-gather | bytes 786432 | tf_op jit(solution)/shard_map/all_gather | solution.py:37
  21.7 8.4 %all_gather.13 = bf16[512,512]{1,0:T(8,128)(2,1)S(1)} all-gather(bf16[256,512]{1,0:T(8,128)(2,1)} %param.11), channel_id=1, replica_groups=mesh['grp'=4,'ep'=4,'sq'=2] {'sq'}, dimensions={0}, use_global_device_ids=true | all-gather | bytes 786432 | tf_op jit(solution)/shard_map/all_gather | solution.py:38
  30.0 1.0 copy.20
  31.0 1.8 reshape.173
  32.8 0.2 fusion.25
  33.0 2.7 fusion
  35.8 0.0 copy-start.2
  35.8 2.0 fusion.1
  37.8 0.0 copy-start.3
  37.8 2.5 multiply_reduce_fusion
  40.3 1.3 fusion.13
  41.7 1.5 copy.22
  43.1 2.6 broadcast_in_dim.51
  45.8 4.1 %reshape.185 = bf16[512,2048]{1,0:T(8,128)(2,1)} reshape(bf16[256,2,2048]{2,1,0:T(2,128)(2,1)} %broadcast_in_dim.51) | data formatting | bytes 4194304 | tf_op jit(solution)/shard_map/reshape | solution.py:71
  49.9 6.7 %scatter_custom_fusion = bf16[768,2048]{1,0:T(8,128)(2,1)} fusion(s32[512]{0:T(512)S(1)} %bitcast.79, bf16[512,2048]{1,0:T(8,128)(2,1)} %reshape.185, bf16[]{:T(256)} %constant.25.clone.1), kind=kCustom, calls=%fused_computation.23 | custom fusion | bytes 3146240 | tf_op jit(solution)/shard_map/scatter | solution.py:78
  56.6 74.8 %all_to_all.10 = bf16[4,192,2048]{2,1,0:T(8,128)(2,1)} all-to-all(bf16[4,192,2048]{2,1,0:T(8,128)(2,1)} %bitcast.72), channel_id=1, replica_groups=mesh['grp'=4,'ep'=4,'sq'=2] {'ep'}, dimensions={0} | all-to-all | bytes 6291456 | tf_op jit(solution)/shard_map/all_to_all | solution.py:86
  131.4 0.0 all-gather.3.cloned.1.call-update
  131.4 0.0 all-gather.5.cloned.1.call-start
  131.5 0.6 copy-done.4
  132.1 0.1 copy.23
  132.2 0.1 mul.89
  132.4 0.1 copy-done.1
  132.5 2.0 broadcast_in_dim.53
  134.4 3.7 %convert_element_type.40 = f32[512,1024]{1,0:T(8,128)} reshape(f32[256,2,1024]{2,1,0:T(2,128)} %broadcast_in_dim.53) | data formatting | bytes 4194304 | tf_op jit(solution)/shard_map/convert_element_type | solution.py:73
  138.1 5.3 %scatter_custom_fusion.1 = bf16[768,1024]{1,0:T(8,128)(2,1)} fusion(s32[512]{0:T(512)S(1)} %bitcast.80, f32[512,1024]{1,0:T(8,128)} %convert_element_type.40, f32[512]{0:T(512)S(1)} %mul.89, bf16[]{:T(256)} %constant.25.clone.1), kind=kCustom, calls=%fused_computation.25 | custom fusion | flops 1048576 | bytes 3672066 | tf_op jit(solution)/shard_map/scatter | solution.py:81
  143.4 40.3 %all_to_all.11 = bf16[4,192,1024]{2,1,0:T(8,128)(2,1)} all-to-all(bf16[4,192,1024]{2,1,0:T(8,128)(2,1)} %bitcast.74), channel_id=1, replica_groups=mesh['grp'=4,'ep'=4,'sq'=2] {'ep'}, dimensions={0} | all-to-all | bytes 3145728 | tf_op jit(solution)/shard_map/all_to_all | solution.py:87
  183.7 0.0 all-gather.5.cloned.1.call-update
  183.7 0.0 reduce-scatter.2.cloned.1.call-start
  183.7 26.9 %all-gather.3.cloned.1.call-done = bf16[1536,2048]{1,0:T(8,128)(2,1)} async-done(((bf16[768,2048]{1,0:T(8,128)(2,1)}), bf16[1536,2048]{1,0:T(8,128)(2,1)}) %all-gather.3.cloned.1.call-update) | async-done | bytes 6291472 | tf_op jit(solution)/shard_map/all_gather | solution.py:95
  210.7 8.5 %fusion.9 = f32[1536,512]{1,0:T(8,128)} fusion(bf16[1536,2048]{1,0:T(8,128)(2,1)} %all-gather.3.cloned.1.call-done, bf16[1,2048,512]{2,1,0:T(8,128)(2,1)} %param.16), kind=kOutput, calls=%fused_computation.14 | convolution fusion | flops 3221225472 | bytes 11534336 | tf_op jit(solution)/shard_map/dot_general | solution.py:14
  219.2 38.0 %all-gather.5.cloned.1.call-done = bf16[1536,1024]{1,0:T(8,128)(2,1)} async-done(((bf16[768,1024]{1,0:T(8,128)(2,1)}), bf16[1536,1024]{1,0:T(8,128)(2,1)}) %all-gather.5.cloned.1.call-update) | async-done | bytes 3145744 | tf_op jit(solution)/shard_map/all_gather | solution.py:96
  257.2 14.6 %fusion.8 = bf16[1,2048,512]{2,1,0:T(8,128)(2,1)} fusion(bf16[1536,2048]{1,0:T(8,128)(2,1)} %all-gather.3.cloned.1.call-done, f32[1536,512]{1,0:T(8,128)} %fusion.9, bf16[1,2048,512]{2,1,0:T(8,128)(2,1)S(1)} %copy-done, bf16[1536,1024]{1,0:T(8,128)(2,1)} %all-gather.5.cloned.1.call-done, s32[]{:T(128)S(6)} %select_n.44), kind=kOutput, calls=%fused_computation.13 | convolution fusion | flops 6452150272 | bytes 21495812 | tf_op jit(solution)/shard_map/dot_general | solution.py:19
  271.8 0.0 reduce-scatter.2.cloned.1.call-update
  271.8 31.6 %reduce-scatter.2.cloned.1.call-done = bf16[1,512,512]{2,1,0:T(8,128)(2,1)} async-done(((bf16[1,2048,512]{2,1,0:T(8,128)(2,1)}), bf16[1,512,512]{2,1,0:T(8,128)(2,1)}) %reduce-scatter.2.cloned.1.call-update) | async-done | bytes 524304 | tf_op jit(solution)/shard_map/reduce_scatter | solution.py:99
  303.4 2.1 convert_element_type.46
  (13 shorter events, 0.1 us)
Async XLA Ops:
  6.5 250.7 %copy-start = (bf16[1,2048,512]{2,1,0:T(8,128)(2,1)S(1)}, bf16[1,2048,512]{2,1,0:T(8,128)(2,1)}, u32[]{:S(2)}) copy-start(bf16[1,2048,512]{2,1,0:T(8,128)(2,1)} %param.17) | copy-start | bytes 6291460
  6.5 204.1 %all-gather.3.cloned.1.call-start = ((), (), s32[]{:S(2)}) async-start(), calls=%async_computation.3 | async-start | bytes 9437184 | tf_op jit(solution)/shard_map/all_gather | solution.py:95
  35.8 2.0 copy-start.2
  37.8 2.5 copy-start.3
  131.4 0.7 copy-start.4
  131.4 1.1 copy-start.1
  131.4 125.8 %all-gather.5.cloned.1.call-start = ((), (), s32[]{:S(2)}) async-start(), calls=%async_computation.4 | async-start | bytes 4718592 | tf_op jit(solution)/shard_map/all_gather | solution.py:96
  183.7 119.7 %reduce-scatter.2.cloned.1.call-start = ((), (), s32[]{:S(2)}) async-start(), calls=%async_computation.5 | async-start | bytes 2621440 | tf_op jit(solution)/shard_map/reduce_scatter | solution.py:99
Sparse Core Ops, SparseCore 0:
  131.6 79.0 all-gather.2
  212.2 44.9 all-gather.4
  272.0 31.4 reduce-scatter.1
where the time goes:
time: 313 us; the launch traced here: 312 us
  blocking collectives  133 us (42%)
  waiting for transfers between devices  96.5 us (31%)
  matrix products  28.4 us (9%)
  local copies, waits for them, and re-layouts  27 us (9%)
  other arithmetic  13.3 us (4%)
  between operations  13.3 us (4%)
    all_to_all x1, blocking collectives, body(): lax.all_to_all(send_inputs, 'ep', split_axis=0, concat_axis=0, tiled=True)  74.8 us
    all_to_all x1, blocking collectives, body(): lax.all_to_all(send_grad, 'ep', split_axis=0, concat_axis=0, tiled=True)  40.3 us
    all_gather x1, waiting for transfers between devices, body(): grad_rows = lax.all_gather(expert_grad, 'sq', axis=0, tiled=True)  38 us
    reduce_scatter x1, waiting for transfers between devices, body(): lax.psum_scatter(summed[None].astype(jnp.bfloat16), 'grp', scatter_dimens...  31.6 us
    all_gather x1, waiting for transfers between devices, body(): input_rows = lax.all_gather(expert_inputs, 'sq', axis=0, tiled=True)  26.9 us
    dot_general x1, matrix products, gate_term(): lax.dot_general(inputs, delta_gate, (((0,), (0,)), ((), ())), preferred_e...  14.6 us
    all_gather x1, blocking collectives, body(): key_rows = lax.all_gather(keys, 'sq', axis=0, tiled=True)  10 us
    dot_general x1, matrix products, gate_term(): pre_gate = jnp.dot(inputs, weight_gate, preferred_element_type=jnp.float32)  8.55 us
  transfers between devices with their start and end apart: 3, of which 3 were waited for; matrix products, arithmetic and copies ran while one was open for 6% of the time, Pallas kernels for 0%

commit v1 on v0

--- a/solution.py
+++ b/solution.py
@@ -3,6 +3,7 @@
 import jax.numpy as jnp
 from jax import lax
 from jax.sharding import PartitionSpec as P
+from jax.lax import all_to_all, axis_size
 
 HEAD_DIM = 128
 LENGTH = 512
@@ -35,7 +36,10 @@
     query_heads = queries.reshape(rows_here, kv_heads, group_size, HEAD_DIM)
     running_max = jnp.full((rows_here, kv_heads, group_size), masked_score, jnp.float32)
     key_rows = lax.all_gather(keys, "sq", axis=0, tiled=True)
-    value_rows = lax.all_gather(values, "sq", axis=0, tiled=True)
+    entries = []
+    for _ in range(axis_size("sq")):
+        entries.append(values)
+    value_rows = jnp.concatenate(all_to_all(jnp.stack(entries, axis=0), "sq", 0, 0), axis=0)
     key_count = key_rows.shape[0]
     key_heads = key_rows.reshape(key_count, kv_heads, HEAD_DIM)
     value_heads = value_rows.reshape(key_count, kv_heads, HEAD_DIM)

time: 313 us -> 315 us (level)
  blocking collectives: 133 us -> 127 us
  starting transfers between devices: 0.09 us -> 4.35 us
    all_gather x1 -> x0, blocking collectives: 8.37 us -> none  [body(): value_rows = lax.all_gather(values, 'sq', axis=0, tiled=True)]
    all_to_all x0 -> x1, starting transfers between devices: none -> 4.23 us  [body(): all_to_all(jnp.stack(entries, axis=0), 'sq', 0, 0)]
  transfers between devices with their start and end apart: 3 -> 4, of which waited for: 3 -> 3; matrix products, arithmetic and copies ran while one was open for 6% -> 10% of each run, Pallas kernels for 0% -> 0%
where the time goes in v1:
time: 315 us
  blocking collectives  127 us (40%)
  waiting for transfers between devices  95.2 us (30%)
  matrix products  30.6 us (10%)
  local copies, waits for them, and re-layouts  28.5 us (9%)
  other arithmetic  15.2 us (5%)
  between operations  13.3 us (4%)
  starting transfers between devices  4.35 us (1%)
    all_to_all x1, blocking collectives, body(): lax.all_to_all(send_inputs, 'ep', split_axis=0, concat_axis=0, tiled=True)  76.1 us
    all_to_all x1, blocking collectives, body(): lax.all_to_all(send_grad, 'ep', split_axis=0, concat_axis=0, tiled=True)  40.9 us
    all_gather x1, waiting for transfers between devices, body(): grad_rows = lax.all_gather(expert_grad, 'sq', axis=0, tiled=True)  38 us
    reduce_scatter x1, waiting for transfers between devices, body(): lax.psum_scatter(summed[None].astype(jnp.bfloat16), 'grp', scatter_dimens...  31.6 us
    all_gather x1, waiting for transfers between devices, body(): input_rows = lax.all_gather(expert_inputs, 'sq', axis=0, tiled=True)  25.6 us
    dot_general x1, matrix products, gate_term(): lax.dot_general(inputs, delta_gate, (((0,), (0,)), ((), ())), preferred_e...  14.6 us
    all_gather x1, blocking collectives, body(): key_rows = lax.all_gather(keys, 'sq', axis=0, tiled=True)  10.5 us
    dot_general x1, matrix products, gate_term(): pre_gate = jnp.dot(inputs, weight_gate, preferred_element_type=jnp.float32)  8.55 us
  transfers between devices with their start and end apart: 4, of which 3 were waited for; matrix products, arithmetic and copies ran while one was open for 10% of the time, Pallas kernels for 0%

profile of v1, /device:TPU:0, one launch (start us, length us, event | category | flops | bytes accessed | tf_op | source)
XLA Modules:
  0.0 314.6 jit_solution(3002747873878759565)
XLA Ops:
  6.5 2.0 pad_maximum_fusion
  8.6 4.2 %all-to-all-start = ((bf16[2,256,512]{2,1,0:T(8,128)(2,1)}), bf16[2,256,512]{2,1,0:T(8,128)(2,1)}, u32[]{:S(2)}, u32[]{:S(2)}) async-start(bf16[2,256,512]{2,1,0:T(8,128)(2,1)} %pad_maximum_fusion), calls=%async_computation | async-start | bytes 1048576 | tf_op jit(solution)/shard_map/all_to_all | solution.py:42
  12.8 0.0 all-gather.3.cloned.1.call-start
  12.8 0.7 broadcast_multiply_fusion
  13.5 0.8 copy.15
  14.3 0.1 eq.46
  14.5 0.1 eq.42
  14.7 1.2 reduce-window.6
  15.9 0.2 slice_reduce_fusion
  16.1 0.2 reduce-window.9
  16.3 0.1 add_bitcast_fusion
  16.4 1.1 copy.18
  17.5 10.5 %all_gather.9 = bf16[512,512]{0,1:T(8,128)(2,1)} all-gather(bf16[256,512]{0,1:T(8,128)(2,1)S(1)} %copy.18), channel_id=1, replica_groups=mesh['grp'=4,'ep'=4,'sq'=2] {'sq'}, dimensions={0}, use_global_device_ids=true | all-gather | bytes 786432 | tf_op jit(solution)/shard_map/all_gather | solution.py:38
  28.0 1.8 reshape.170
  29.8 0.2 fusion.26
  29.9 2.7 fusion
  32.7 2.0 fusion.1
  34.8 1.1 copy-done.1
  35.9 0.1 copy.14
  36.0 0.1 mul.78
  36.2 1.2 reshape.195
  37.4 0.0 copy-start.3
  37.4 4.7 %multiply_reduce_fusion = (f32[256]{0:T(256)S(1)}, f32[256,4,4,128]{0,3,2,1:T(8,128)S(1)}) fusion(f32[256,4,4]{0,2,1:T(4,128)S(1)} %fusion.1, f32[4,512,256,4]{2,1,3,0:T(8,128)} %copy-done.1, f32[256,4,4]{0,2,1:T(4,128)S(1)} %broadcast_maximum_fusion, pred[256,512]{0,1:T(8,128)(4,1)S(1)} %fusion.26, bf16[512,4,128,1]{2,1,0,3:T(4,128)(2,1)S(1)} %bitcast.72), kind=kOutput, calls=%fused_computation.22 | convolution fusion | flops 548929280 | bytes 11174912 | tf_op jit(solution)/shard_map/tkgr,rkd->tkgd/dot_general | solution.py:58
  42.2 1.3 fusion.13
  43.5 1.5 copy.22
  45.0 2.6 broadcast_in_dim.51
  47.6 4.1 %reshape.181 = bf16[512,2048]{1,0:T(8,128)(2,1)} reshape(bf16[256,2,2048]{2,1,0:T(2,128)(2,1)} %broadcast_in_dim.51) | data formatting | bytes 4194304 | tf_op jit(solution)/shard_map/reshape | solution.py:75
  51.7 6.7 %scatter_custom_fusion = bf16[768,2048]{1,0:T(8,128)(2,1)} fusion(s32[512]{0:T(512)S(1)} %bitcast.76, bf16[512,2048]{1,0:T(8,128)(2,1)} %reshape.181, bf16[]{:T(256)} %constant.25.clone.1), kind=kCustom, calls=%fused_computation.23 | custom fusion | bytes 3146240 | tf_op jit(solution)/shard_map/scatter | solution.py:82
  58.4 76.1 %all_to_all.15 = bf16[4,192,2048]{2,1,0:T(8,128)(2,1)} all-to-all(bf16[4,192,2048]{2,1,0:T(8,128)(2,1)} %bitcast.68), channel_id=1, replica_groups=mesh['grp'=4,'ep'=4,'sq'=2] {'ep'}, dimensions={0} | all-to-all | bytes 6291456 | tf_op jit(solution)/shard_map/all_to_all | solution.py:90
  134.6 0.0 all-gather.3.cloned.1.call-update
  134.6 0.0 all-gather.5.cloned.1.call-start
  134.6 0.6 copy-done.4
  135.2 0.1 copy.23
  135.4 0.1 mul.89
  135.5 0.1 copy-done.2
  135.6 2.0 broadcast_in_dim.53
  137.6 3.8 %convert_element_type.40 = f32[512,1024]{1,0:T(8,128)} reshape(f32[256,2,1024]{2,1,0:T(2,128)} %broadcast_in_dim.53) | data formatting | bytes 4194304 | tf_op jit(solution)/shard_map/convert_element_type | solution.py:77
  141.4 5.3 %scatter_custom_fusion.1 = bf16[768,1024]{1,0:T(8,128)(2,1)} fusion(s32[512]{0:T(512)S(1)} %bitcast.77, f32[512,1024]{1,0:T(8,128)} %convert_element_type.40, f32[512]{0:T(512)S(1)} %mul.89, bf16[]{:T(256)} %constant.25.clone.1), kind=kCustom, calls=%fused_computation.25 | custom fusion | flops 1048576 | bytes 3672066 | tf_op jit(solution)/shard_map/scatter | solution.py:85
  146.7 40.9 %all_to_all.16 = bf16[4,192,1024]{2,1,0:T(8,128)(2,1)} all-to-all(bf16[4,192,1024]{2,1,0:T(8,128)(2,1)} %bitcast.70), channel_id=1, replica_groups=mesh['grp'=4,'ep'=4,'sq'=2] {'ep'}, dimensions={0} | all-to-all | bytes 3145728 | tf_op jit(solution)/shard_map/all_to_all | solution.py:91
  187.5 0.0 all-gather.5.cloned.1.call-update
  187.6 0.0 reduce-scatter.2.cloned.1.call-start
  187.6 25.6 %all-gather.3.cloned.1.call-done = bf16[1536,2048]{1,0:T(8,128)(2,1)} async-done(((bf16[768,2048]{1,0:T(8,128)(2,1)}), bf16[1536,2048]{1,0:T(8,128)(2,1)}) %all-gather.3.cloned.1.call-update) | async-done | bytes 6291472 | tf_op jit(solution)/shard_map/all_gather | solution.py:99
  213.2 8.5 %fusion.9 = f32[1536,512]{1,0:T(8,128)} fusion(bf16[1536,2048]{1,0:T(8,128)(2,1)} %all-gather.3.cloned.1.call-done, bf16[1,2048,512]{2,1,0:T(8,128)(2,1)} %param.16), kind=kOutput, calls=%fused_computation.14 | convolution fusion | flops 3221225472 | bytes 11534336 | tf_op jit(solution)/shard_map/dot_general | solution.py:15
  221.8 38.0 %all-gather.5.cloned.1.call-done = bf16[1536,1024]{1,0:T(8,128)(2,1)} async-done(((bf16[768,1024]{1,0:T(8,128)(2,1)}), bf16[1536,1024]{1,0:T(8,128)(2,1)}) %all-gather.5.cloned.1.call-update) | async-done | bytes 3145744 | tf_op jit(solution)/shard_map/all_gather | solution.py:100
  259.7 14.6 %fusion.8 = bf16[1,2048,512]{2,1,0:T(8,128)(2,1)} fusion(bf16[1536,2048]{1,0:T(8,128)(2,1)} %all-gather.3.cloned.1.call-done, f32[1536,512]{1,0:T(8,128)} %fusion.9, bf16[1,2048,512]{2,1,0:T(8,128)(2,1)S(1)} %copy-done, bf16[1536,1024]{1,0:T(8,128)(2,1)} %all-gather.5.cloned.1.call-done, s32[]{:T(128)S(6)} %select_n.44), kind=kOutput, calls=%fused_computation.13 | convolution fusion | flops 6452150272 | bytes 21495812 | tf_op jit(solution)/shard_map/dot_general | solution.py:20
  274.3 0.0 reduce-scatter.2.cloned.1.call-update
  274.4 31.6 %reduce-scatter.2.cloned.1.call-done = bf16[1,512,512]{2,1,0:T(8,128)(2,1)} async-done(((bf16[1,2048,512]{2,1,0:T(8,128)(2,1)}), bf16[1,512,512]{2,1,0:T(8,128)(2,1)}) %reduce-scatter.2.cloned.1.call-update) | async-done | bytes 524304 | tf_op jit(solution)/shard_map/reduce_scatter | solution.py:103
  305.9 2.1 convert_element_type.46
  (15 shorter events, 0.1 us)
Async XLA Ops:
  6.5 253.2 %copy-start = (bf16[1,2048,512]{2,1,0:T(8,128)(2,1)S(1)}, bf16[1,2048,512]{2,1,0:T(8,128)(2,1)}, u32[]{:S(2)}) copy-start(bf16[1,2048,512]{2,1,0:T(8,128)(2,1)} %param.17) | copy-start | bytes 6291460
  8.6 27.6 %all-to-all-start = ((bf16[2,256,512]{2,1,0:T(8,128)(2,1)}), bf16[2,256,512]{2,1,0:T(8,128)(2,1)}, u32[]{:S(2)}, u32[]{:S(2)}) async-start(bf16[2,256,512]{2,1,0:T(8,128)(2,1)} %pad_maximum_fusion), calls=%async_computation | async-start | bytes 1048576 | tf_op jit(solution)/shard_map/all_to_all | solution.py:42
  12.8 200.4 %all-gather.3.cloned.1.call-start = ((), (), s32[]{:S(2)}) async-start(), calls=%async_computation.4 | async-start | bytes 9437184 | tf_op jit(solution)/shard_map/all_gather | solution.py:99
  32.7 3.2 %copy-start.1 = (f32[4,512,256,4]{2,1,3,0:T(8,128)}, f32[4,512,256,4]{2,1,3,0:T(8,128)S(1)}, u32[]{:S(2)}) copy-start(f32[4,512,256,4]{2,1,3,0:T(8,128)S(1)} %get-tuple-element.6) | copy-start | bytes 25165828
  37.4 4.8 %copy-start.3 = (f32[2048]{0:T(1024)S(1)}, f32[2048]{0:T(1024)}, u32[]{:S(2)}) copy-start(f32[2048]{0:T(1024)} %param.12) | copy-start | bytes 24580
  134.6 0.7 copy-start.4
  134.6 1.1 copy-start.2
  134.6 125.1 %all-gather.5.cloned.1.call-start = ((), (), s32[]{:S(2)}) async-start(), calls=%async_computation.5 | async-start | bytes 4718592 | tf_op jit(solution)/shard_map/all_gather | solution.py:100
  187.6 118.4 %reduce-scatter.2.cloned.1.call-start = ((), (), s32[]{:S(2)}) async-start(), calls=%async_computation.6 | async-start | bytes 2621440 | tf_op jit(solution)/shard_map/reduce_scatter | solution.py:103
Sparse Core Ops, SparseCore 0:
  134.7 78.4 all-gather.2
  214.8 44.9 all-gather.4
  274.5 31.4 reduce-scatter.1
